TPU v7x, 256 devices: a whole 4x4x8 slice. The times are simulated.
256 devices in a mesh: lat: 16 (over y, x), kpt: 16 (over z, core).
Axes of the slice: x: 4, y: 4, z: 8, core: 2. Of those that a mesh axis runs over, the one named last changes fastest.
Arguments:
- coarse: bfloat16 [2, 16, 256, 12288], P(None, 'lat', 'kpt'), may hold values from -0.1875 to 0.1875
- rp_vectors: int32 [16, 3], P('lat'), may hold values from -4 to 4
- rp_weights: int32 [16], P('lat'), may hold values from 1 to 3
- re_vectors: int32 [256, 3], replicated, may hold values from -4 to 4
- re_weights: int32 [256], replicated, may hold values from 1 to 3
- q_points: float32 [2, 3], replicated, may hold values from 0 to 1
- k_points: float32 [1024, 3], P('kpt'), may hold values from 0 to 1
- modes_rot: bfloat16 [2, 2, 48, 48], replicated, may hold values from -0.625 to 0.625
- u_k: bfloat16 [2, 1024, 16, 16], P(None, 'kpt'), may hold values from -1 to 1
- u_kq: bfloat16 [2, 2, 1024, 16, 16], P(None, None, 'kpt'), may hold values from -1 to 1
- mask_k: int32 [1024, 16], P('kpt'), may hold values 0 or 1
- mask_kq: int32 [2, 1024, 16], P(None, 'kpt'), may hold values 0 or 1
Outputs:
- coupling: bfloat16 [2, 1024, 2, 12288], P(None, 'kpt', None, 'lat')
All inputs are finite; a program needn't handle non-finite values. No bound on the sum of `mask_k` or of `mask_kq` on one device may be relied on, other than what follows from the above.
Results may differ from a plain program's by a relative error of at most 0.017.
Values may be sent and summed in bfloat16 or wider, within the bound.
No kernel may reach another device: no remote copies, remote signals or barrier semaphores. Data moves between devices by JAX's collectives and lax.ppermute only.
A program may use at most 64 MiB of HBM per device.

v0:
```python
import jax
import jax.numpy as jnp
from jax import lax
from jax.sharding import PartitionSpec as P

two_pi = 6.283185307179586


def phases(points, vectors, weights):
    cells = vectors.astype(jnp.float32)
    argument = two_pi * (
        points[:, 0:1] * cells[None, :, 0]
        + points[:, 1:2] * cells[None, :, 1]
        + points[:, 2:3] * cells[None, :, 2]
    )
    inverse = 1.0 / weights.astype(jnp.float32)
    return (
        (jnp.cos(argument) * inverse).astype(jnp.bfloat16),
        (jnp.sin(argument) * inverse).astype(jnp.bfloat16),
    )


def rotate_modes(values, modes_rot):
    shape = values.shape
    mode_count = modes_rot.shape[2]
    split = values.reshape(shape[0], shape[1], shape[2], mode_count, shape[3] // mode_count)
    br = jnp.einsum(
        "qmn,qrmx->qrnx", modes_rot[0], split[0], preferred_element_type=jnp.float32
    ) - jnp.einsum("qmn,qrmx->qrnx", modes_rot[1], split[1], preferred_element_type=jnp.float32)
    bi = jnp.einsum(
        "qmn,qrmx->qrnx", modes_rot[0], split[1], preferred_element_type=jnp.float32
    ) + jnp.einsum("qmn,qrmx->qrnx", modes_rot[1], split[0], preferred_element_type=jnp.float32)
    return jnp.stack([br, bi]).reshape(shape).astype(jnp.bfloat16)


def phonon_sum(block, vectors, weights, q_points):
    phase_real, phase_imag = phases(q_points, vectors, weights)
    rows = block.shape[1]
    cells = block.shape[2]
    lanes = block.shape[3]
    flat_real = block[0].reshape(rows, cells * lanes)
    flat_imag = block[1].reshape(rows, cells * lanes)
    part_real = jnp.dot(phase_real, flat_real, preferred_element_type=jnp.float32) - jnp.dot(
        phase_imag, flat_imag, preferred_element_type=jnp.float32
    )
    part_imag = jnp.dot(phase_real, flat_imag, preferred_element_type=jnp.float32) + jnp.dot(
        phase_imag, flat_real, preferred_element_type=jnp.float32
    )
    return jnp.stack([part_real, part_imag]).reshape(2, q_points.shape[0], cells, lanes)


def per_device(
    coarse,
    rp_vectors,
    rp_weights,
    re_vectors,
    re_weights,
    q_points,
    k_points,
    modes_rot,
    u_k,
    u_kq,
    mask_k,
    mask_kq,
):
    q_count = q_points.shape[0]
    k_count = k_points.shape[0]
    band_count = u_k.shape[2]
    partial_value = phonon_sum(coarse, rp_vectors, rp_weights, q_points)
    summed = lax.psum_scatter(partial_value, "lat", scatter_dimension=2, tiled=True).astype(
        jnp.bfloat16
    )
    rotated = rotate_modes(summed, modes_rot)
    shared = lax.all_to_all(rotated, "lat", split_axis=3, concat_axis=2, tiled=True)
    lane_local = shared.shape[3]
    portion = lax.all_gather(shared, "kpt", axis=2, tiled=True)
    kreal, kimag = phases(k_points, re_vectors, re_weights)
    er = jnp.einsum(
        "kr,qrx->kqx", kreal, portion[0], preferred_element_type=jnp.float32
    ) - jnp.einsum("kr,qrx->kqx", kimag, portion[1], preferred_element_type=jnp.float32)
    ei = jnp.einsum(
        "kr,qrx->kqx", kreal, portion[1], preferred_element_type=jnp.float32
    ) + jnp.einsum("kr,qrx->kqx", kimag, portion[0], preferred_element_type=jnp.float32)
    totals = jnp.stack([er, ei])
    mode_local = lane_local // (band_count * band_count)
    field = totals.astype(jnp.bfloat16).reshape(
        2, k_count, q_count, mode_local, band_count, band_count
    )
    tr = jnp.einsum(
        "kqmab,kbn->kqman", field[0], u_k[0], preferred_element_type=jnp.float32
    ) - jnp.einsum("kqmab,kbn->kqman", field[1], u_k[1], preferred_element_type=jnp.float32)
    ti = jnp.einsum(
        "kqmab,kbn->kqman", field[0], u_k[1], preferred_element_type=jnp.float32
    ) + jnp.einsum("kqmab,kbn->kqman", field[1], u_k[0], preferred_element_type=jnp.float32)
    tr = tr.astype(jnp.bfloat16)
    ti = ti.astype(jnp.bfloat16)
    outr = jnp.einsum(
        "qkac,kqman->kqmcn", u_kq[0], tr, preferred_element_type=jnp.float32
    ) + jnp.einsum("qkac,kqman->kqmcn", u_kq[1], ti, preferred_element_type=jnp.float32)
    outi = jnp.einsum(
        "qkac,kqman->kqmcn", u_kq[0], ti, preferred_element_type=jnp.float32
    ) - jnp.einsum("qkac,kqman->kqmcn", u_kq[1], tr, preferred_element_type=jnp.float32)
    window = (
        jnp.transpose(mask_kq.astype(jnp.float32), (1, 0, 2))[:, :, None, :, None]
        * mask_k.astype(jnp.float32)[:, None, None, None, :]
    )
    result = jnp.stack([outr * window, outi * window])
    return result.reshape(2, k_count, q_count, lane_local).astype(jnp.bfloat16)


def solution(mesh):
    placed = (
        P(None, "lat", "kpt", None),
        P("lat", None),
        P("lat"),
        P(),
        P(),
        P(),
        P("kpt", None),
        P(),
        P(None, "kpt", None, None),
        P(None, None, "kpt", None, None),
        P("kpt", None),
        P(None, "kpt", None),
    )
    return jax.shard_map(
        per_device,
        mesh=mesh,
        in_specs=placed,
        out_specs=P(None, "kpt", None, "lat"),
        check_vma=False,
    )
```

profile of v0, /device:TPU:1, one launch (start us, length us, event | category | flops | bytes accessed | tf_op | source)
XLA Modules:
  0.0 256.3 jit_solution(5092199044945277099)
XLA Ops:
  7.2 0.7 convert_element_type.53
  7.8 0.6 fusion.56
  8.5 1.2 convert_bitcast_fusion.1
  10.1 0.3 copy-done.10
  10.4 2.1 convert_reduce_fusion.1
  12.4 1.5 multiply_subtract_fusion
  13.9 1.4 pad_maximum_fusion
  15.4 86.5 %all-reduce.2 = bf16[2,2,16,12288]{3,1,2,0:T(2,128)(2,1)} all-reduce(f32[2,2,16,12288]{3,1,2,0:T(2,128)S(1)} %pad_maximum_fusion), channel_id=2, replica_groups=mesh['lat'=16,'kpt'=16] {'lat'}, use_global_device_ids=true, to_apply=%region_0.0.clone | all-reduce | flops 786432 | bytes 4718592
  101.9 0.6 dynamic-slice
  102.5 1.6 dynamic-slice_convert_fusion
  104.6 0.2 fusion.4
  104.8 0.2 fusion.5
  105.1 10.0 %copy.99 = bf16[2,2,1,12288]{1,0,2,3:T(2,128)(2,1)} copy(bf16[2,2,1,12288]{3,1,2,0:T(2,128)(2,1)S(1)} %pad_maximum_fusion.2) | data formatting | bytes 196608 | tf_op jit(solution)/shard_map/stack | solution.py:33
  115.1 13.7 %reshape.158 = bf16[16,2,1536]{2,1,0:T(2,128)(2,1)S(1)} reshape(bf16[12288,1,2,2]{3,2,1,0:T(2,128)(2,1)} %bitcast.147) | data formatting | bytes 196608
  128.8 9.2 %all_to_all.12 = bf16[16,2,1536]{2,1,0:T(2,128)(2,1)S(1)} all-to-all(bf16[16,2,1536]{2,1,0:T(2,128)(2,1)S(1)} %reshape.158), channel_id=1, replica_groups=mesh['lat'=16,'kpt'=16] {'lat'}, dimensions={0} | all-to-all | bytes 196608 | tf_op jit(solution)/shard_map/all_to_all | solution.py:74
  138.0 14.7 %reshape.159 = bf16[12288,1,2,2]{3,2,1,0:T(2,128)(2,1)} reshape(bf16[16,2,1536]{2,1,0:T(2,128)(2,1)S(1)} %all_to_all.12) | data formatting | bytes 196608
  152.8 9.9 %copy.128 = bf16[2,2,16,768]{3,2,1,0:T(8,128)(2,1)} copy(bf16[2,2,16,768]{1,0,3,2:T(2,128)(2,1)} %bitcast.148) | data formatting | bytes 196608 | tf_op jit(solution)/shard_map/all_to_all | solution.py:74
  162.8 0.3 copy.133
  163.0 1.0 copy.134
  164.0 1.5 copy.136
  165.5 1.5 copy.135
  167.1 0.7 broadcast_multiply_fusion
  167.8 45.9 %all-gather.2.cloned.1.call-done = bf16[2,2,256,768]{3,2,1,0:T(8,128)(2,1)} async-done(((bf16[2,2,16,768]{3,2,1,0:T(8,128)(2,1)}), bf16[2,2,256,768]{3,2,1,0:T(8,128)(2,1)}) %all-gather.2.cloned.1.call-update) | async-done | bytes 1572880 | tf_op jit(solution)/shard_map/all_gather | solution.py:76
  213.8 1.7 fusion.9
  215.5 1.6 fusion.1
  217.1 0.9 copy.104
  218.1 0.5 fusion.8
  218.6 0.5 fusion
  219.1 0.2 copy.101
  219.3 1.3 copy.103
  220.6 2.2 copy.106
  222.8 1.5 fusion.21
  224.3 0.5 fusion.19
  224.8 0.5 add_convert_fusion
  225.4 0.4 copy-done.4
  225.8 0.6 subtract_convert_fusion
  226.3 0.5 copy-done.2
  226.8 2.4 fusion.10
  229.2 0.6 fusion.16
  229.8 2.3 fusion.14
  232.1 2.3 fusion.12
  234.4 3.4 %copy.118 = f32[64,2,3,16,16]{0,3,4,2,1:T(8,128)} copy(f32[64,2,3,16,16]{4,3,2,1,0:T(8,128)} %fusion.10) | data formatting | bytes 786432 | tf_op jit(solution)/shard_map/qkac,kqman->kqmcn/dot_general | solution.py:102
  237.9 2.3 copy.113
  240.1 3.6 %copy.117 = f32[64,2,3,16,16]{0,3,4,2,1:T(8,128)} copy(f32[64,2,3,16,16]{4,3,2,1,0:T(8,128)} %fusion.14) | data formatting | bytes 786432 | tf_op jit(solution)/shard_map/qkac,kqman->kqmcn/dot_general | solution.py:100
  243.8 2.3 copy.114
  246.1 2.1 fusion.7
  248.1 0.2 pad_maximum_fusion.1
  248.3 1.1 copy.119
  (47 shorter events, 1.0 us)
Async XLA Ops:
  6.5 207.2 %all-gather.2.cloned.1.call-start = ((), (), s32[]{:S(2)}) async-start(), calls=%async_computation.1 | async-start | bytes 1671168 | tf_op jit(solution)/shard_map/all_gather | solution.py:76
  9.7 0.7 copy-start.10
  15.3 86.6 %copy-start.15 = (u32[256]{0:T(256)S(1)}, u32[256]{0:T(256)}, u32[]{:S(2)}) copy-start(u32[256]{0:T(256)} %constant.12) | copy-start | bytes 3076
  15.4 88.8 %copy-start.7 = (bf16[2,2,48,48]{3,2,1,0:T(8,128)(2,1)S(1)}, bf16[2,2,48,48]{3,2,1,0:T(8,128)(2,1)}, u32[]{:S(2)}) copy-start(bf16[2,2,48,48]{3,2,1,0:T(8,128)(2,1)} %param.19) | copy-start | bytes 55300
  152.7 9.9 %copy-start.12 = (s32[256,3]{0,1:T(4,128)S(1)}, s32[256,3]{0,1:T(4,128)}, u32[]{:S(2)}) copy-start(s32[256,3]{0,1:T(4,128)} %param.15) | copy-start | bytes 9220
  152.7 10.0 %copy-start.11 = (s32[64,16]{0,1:T(8,128)S(1)}, s32[64,16]{0,1:T(8,128)}, u32[]{:S(2)}) copy-start(s32[64,16]{0,1:T(8,128)} %param.22) | copy-start | bytes 12292
  152.8 10.0 %copy-start.8 = (bf16[2,64,16,16]{1,3,2,0:T(8,128)(2,1)S(1)}, bf16[2,64,16,16]{1,3,2,0:T(8,128)(2,1)}, u32[]{:S(2)}) copy-start(bf16[2,64,16,16]{1,3,2,0:T(8,128)(2,1)} %param.20) | copy-start | bytes 196612
  152.8 11.2 %copy-start.6 = (bf16[2,2,64,16,16]{2,4,3,1,0:T(8,128)(2,1)S(1)}, bf16[2,2,64,16,16]{2,4,3,1,0:T(8,128)(2,1)}, u32[]{:S(2)}) copy-start(bf16[2,2,64,16,16]{2,4,3,1,0:T(8,128)(2,1)} %param.21) | copy-start | bytes 393220
  162.6 4.4 %copy-start.14 = (s32[256]{0:T(256)S(1)}, s32[256]{0:T(256)}, u32[]{:S(2)}) copy-start(s32[256]{0:T(256)} %param.16) | copy-start | bytes 3076
  162.7 4.4 %copy-start.13 = (f32[64,3]{0,1:T(4,128)S(1)}, f32[64,3]{0,1:T(4,128)}, u32[]{:S(2)}) copy-start(f32[64,3]{0,1:T(4,128)} %param.18) | copy-start | bytes 2308
  162.7 4.5 %copy-start.9 = (s32[2,64,16]{1,2,0:T(8,128)S(1)}, s32[2,64,16]{1,2,0:T(8,128)}, u32[]{:S(2)}) copy-start(s32[2,64,16]{1,2,0:T(8,128)} %param.23) | copy-start | bytes 24580
  213.7 4.3 %copy-start.1 = (bf16[2,2,256,768]{3,2,1,0:T(8,128)(2,1)S(1)}, bf16[2,2,256,768]{3,2,1,0:T(8,128)(2,1)}, u32[]{:S(2)}) copy-start(bf16[2,2,256,768]{3,2,1,0:T(8,128)(2,1)} %all-gather.2.cloned.1.call-done) | copy-start | bytes 4718596
  224.8 1.0 copy-start.4
  225.8 1.0 copy-start.2
  226.8 2.4 copy-start.3
  240.1 3.6 %copy-start = (f32[64,2,3,16,16]{4,3,2,1,0:T(8,128)S(1)}, f32[64,2,3,16,16]{4,3,2,1,0:T(8,128)}, u32[]{:S(2)}) copy-start(f32[64,2,3,16,16]{4,3,2,1,0:T(8,128)} %fusion.12) | copy-start | bytes 1179652
  243.8 2.3 copy-start.5
Sparse Core Ops, SparseCore 0:
  162.8 50.9 all-gather.1
where the time goes:
time: 257 us; the launch traced here: 256 us
  blocking collectives  95.8 us (37%)
  local copies, waits for them, and re-layouts  74.4 us (29%)
  waiting for transfers between devices  45.9 us (18%)
  matrix products  15.8 us (6%)
  between operations  14.4 us (6%)
  other arithmetic  9.95 us (4%)
    unnamed x1, blocking collectives  86.5 us
    all_gather x1, waiting for transfers between devices, per_device(): portion = lax.all_gather(shared, 'kpt', axis=2, tiled=True)  45.9 us
    unnamed x41, local copies, waits for them, and re-layouts  34.8 us
    another operation x3, local copies, waits for them, and re-layouts, rotate_modes(): return jnp.stack([br, bi]).reshape(shape).astype(jnp.bfloat16)  10 us
    all_to_all x1, local copies, waits for them, and re-layouts, per_device(): lax.all_to_all(rotated, 'lat', split_axis=3, concat_axis=2, tiled=True)  9.89 us
    all_to_all x1, blocking collectives, per_device(): lax.all_to_all(rotated, 'lat', split_axis=3, concat_axis=2, tiled=True)  9.25 us
  transfers between devices with their start and end apart: 1, of which 1 were waited for; matrix products, arithmetic and copies ran while one was open for 2% of the time, Pallas kernels for 0%

commit v1 on v0

--- a/solution.py
+++ b/solution.py
@@ -4,6 +4,28 @@
 from jax.sharding import PartitionSpec as P
 
 two_pi = 6.283185307179586
+
+
+def cut_along(value, dim, count):
+    before, after = (value.shape[:dim], value.shape[dim + 1 :])
+    return jnp.moveaxis(value.reshape(*before, count, -1, *after), dim, 0)
+
+
+def joined_along(pieces, dim):
+    pieces = jnp.moveaxis(pieces, 0, dim)
+    shape = pieces.shape
+    return pieces.reshape(*shape[:dim], shape[dim] * shape[dim + 1], *shape[dim + 2 :])
+
+
+def swapped_with_each(x, axis, split_dim, concat_dim):
+    size, index = (lax.axis_size(axis), lax.axis_index(axis))
+    tiles = cut_along(x, split_dim, size)
+    done = [tiles[index]]
+    for turn in range(1, size):
+        sent = tiles[index ^ turn]
+        done.append(lax.ppermute(sent, axis, [(i, i ^ turn) for i in range(size)]))
+    tiles = jnp.stack(done)[index ^ jnp.arange(size)]
+    return joined_along(tiles, concat_dim)
 
 
 def phases(points, vectors, weights):
@@ -71,7 +93,7 @@
         jnp.bfloat16
     )
     rotated = rotate_modes(summed, modes_rot)
-    shared = lax.all_to_all(rotated, "lat", split_axis=3, concat_axis=2, tiled=True)
+    shared = swapped_with_each(rotated, "lat", 3, 2)
     lane_local = shared.shape[3]
     portion = lax.all_gather(shared, "kpt", axis=2, tiled=True)
     kreal, kimag = phases(k_points, re_vectors, re_weights)

time: 257 us -> 268 us (1.043)
  waiting for transfers between devices: 45.9 us -> 104 us
  local copies, waits for them, and re-layouts: 74.4 us -> 28.3 us
  blocking collectives: 95.8 us -> 86.6 us
  starting transfers between devices: 0.01 us -> 8.94 us
    ppermute x0 -> x15, waiting for transfers between devices: none -> 45.9 us  [swapped_with_each(): done.append(lax.ppermute(sent, axis, [(i, i ^ turn) for i in range(size)]))]
    unnamed x41 -> x55, local copies, waits for them, and re-layouts: 34.8 us -> 6.61 us
    all_gather x1, waiting for transfers between devices: 45.9 us -> 57.7 us  [per_device(): portion = lax.all_gather(shared, 'kpt', axis=2, tiled=True)]
    all_to_all x1 -> x0, local copies, waits for them, and re-layouts: 9.89 us -> none  [per_device(): lax.all_to_all(rotated, 'lat', split_axis=3, concat_axis=2, tiled=True)]
    another operation x3, local copies, waits for them, and re-layouts: 10 us -> 0.11 us  [rotate_modes(): return jnp.stack([br, bi]).reshape(shape).astype(jnp.bfloat16)]
    all_to_all x1 -> x0, blocking collectives: 9.25 us -> none  [per_device(): lax.all_to_all(rotated, 'lat', split_axis=3, concat_axis=2, tiled=True)]
    ppermute x0 -> x15, starting transfers between devices: none -> 8.94 us  [swapped_with_each(): done.append(lax.ppermute(sent, axis, [(i, i ^ turn) for i in range(size)]))]
  transfers between devices with their start and end apart: 1 -> 16, of which waited for: 1 -> 12; matrix products, arithmetic and copies ran while one was open for 2% -> 2% of each run, Pallas kernels for 0% -> 0%
where the time goes in v1:
time: 268 us
  waiting for transfers between devices  104 us (39%)
  blocking collectives  86.6 us (32%)
  local copies, waits for them, and re-layouts  28.3 us (11%)
  matrix products  15.8 us (6%)
  between operations  14.6 us (5%)
  other arithmetic  9.93 us (4%)
  starting transfers between devices  8.94 us (3%)
    unnamed x1, blocking collectives  86.6 us
    all_gather x1, waiting for transfers between devices, per_device(): portion = lax.all_gather(shared, 'kpt', axis=2, tiled=True)  57.7 us
    ppermute x15, waiting for transfers between devices, swapped_with_each(): done.append(lax.ppermute(sent, axis, [(i, i ^ turn) for i in range(size)]))  45.9 us
    ppermute x15, starting transfers between devices, swapped_with_each(): done.append(lax.ppermute(sent, axis, [(i, i ^ turn) for i in range(size)]))  8.94 us
    unnamed x55, local copies, waits for them, and re-layouts  6.61 us
  transfers between devices with their start and end apart: 16, of which 12 were waited for; matrix products, arithmetic and copies ran while one was open for 2% of the time, Pallas kernels for 0%

profile of v1, /device:TPU:1, one launch (start us, length us, event | category | flops | bytes accessed | tf_op | source)
XLA Modules:
  0.0 267.7 jit_solution(10935259360231061925)
XLA Ops:
  7.2 0.7 convert_element_type.54
  7.8 0.6 fusion.57
  8.5 1.2 convert_bitcast_fusion.1
  10.4 2.2 convert_reduce_fusion.1
  12.6 1.5 multiply_subtract_fusion
  14.0 1.4 pad_maximum_fusion
  15.5 86.6 %all-reduce.2 = bf16[2,2,16,12288]{3,1,2,0:T(2,128)(2,1)} all-reduce(f32[2,2,16,12288]{3,1,2,0:T(2,128)S(1)} %pad_maximum_fusion), channel_id=3, replica_groups=mesh['lat'=16,'kpt'=16] {'lat'}, use_global_device_ids=true, to_apply=%region_0.0.clone | all-reduce | flops 786432 | bytes 4718592
  102.1 0.6 dynamic-slice.64
  102.7 1.6 dynamic-slice_convert_fusion
  105.5 1.2 collective-permute-start.14
  106.7 0.7 collective-permute-start.13
  107.4 6.0 %collective-permute-start.11 = (bf16[2,2,1,768]{3,1,0,2:T(2,128)(2,1)S(1)}, bf16[2,2,1,768]{3,1,0,2:T(2,128)(2,1)S(1)}, u32[]{:S(2)}, u32[]{:S(2)}) collective-permute-start(bf16[2,2,1,768]{3,1,0,2:T(2,128)(2,1)S(1)} %get-tuple-element.20), channel_id=1, source_target_pairs={{0,192},{16,208},{32,224},{48,240},{64,128},{80,144},{96,160},{112... | collective-permute-start | bytes 18440 | tf_op jit(solution)/shard_map/ppermute | solution.py:26
  113.4 2.4 collective-permute-done
  115.8 4.0 %collective-permute-done.1 = bf16[2,2,1,768]{3,1,0,2:T(2,128)(2,1)S(1)} collective-permute-done((bf16[2,2,1,768]{3,1,0,2:T(2,128)(2,1)S(1)}, bf16[2,2,1,768]{3,1,0,2:T(2,128)(2,1)S(1)}, u32[]{:S(2)}, u32[]{:S(2)}) %collective-permute-start.1) | collective-permute-done | bytes 6176 | tf_op jit(solution)/shard_map/ppermute | solution.py:26
  119.8 3.7 %collective-permute-done.2 = bf16[2,2,1,768]{3,1,0,2:T(2,128)(2,1)S(1)} collective-permute-done((bf16[2,2,1,768]{3,1,0,2:T(2,128)(2,1)S(1)}, bf16[2,2,1,768]{3,1,0,2:T(2,128)(2,1)S(1)}, u32[]{:S(2)}, u32[]{:S(2)}) %collective-permute-start.2) | collective-permute-done | bytes 6176 | tf_op jit(solution)/shard_map/ppermute | solution.py:26
  123.5 2.8 %collective-permute-done.3 = bf16[2,2,1,768]{3,1,0,2:T(2,128)(2,1)S(1)} collective-permute-done((bf16[2,2,1,768]{3,1,0,2:T(2,128)(2,1)S(1)}, bf16[2,2,1,768]{3,1,0,2:T(2,128)(2,1)S(1)}, u32[]{:S(2)}, u32[]{:S(2)}) %collective-permute-start.3) | collective-permute-done | bytes 6176 | tf_op jit(solution)/shard_map/ppermute | solution.py:26
  126.3 3.4 %collective-permute-done.4 = bf16[2,2,1,768]{3,1,0,2:T(2,128)(2,1)S(1)} collective-permute-done((bf16[2,2,1,768]{3,1,0,2:T(2,128)(2,1)S(1)}, bf16[2,2,1,768]{3,1,0,2:T(2,128)(2,1)S(1)}, u32[]{:S(2)}, u32[]{:S(2)}) %collective-permute-start.4) | collective-permute-done | bytes 6176 | tf_op jit(solution)/shard_map/ppermute | solution.py:26
  129.7 4.9 %collective-permute-done.5 = bf16[2,2,1,768]{3,1,0,2:T(2,128)(2,1)S(1)} collective-permute-done((bf16[2,2,1,768]{3,1,0,2:T(2,128)(2,1)S(1)}, bf16[2,2,1,768]{3,1,0,2:T(2,128)(2,1)S(1)}, u32[]{:S(2)}, u32[]{:S(2)}) %collective-permute-start.5) | collective-permute-done | bytes 6176 | tf_op jit(solution)/shard_map/ppermute | solution.py:26
  134.5 4.6 %collective-permute-done.6 = bf16[2,2,1,768]{3,1,0,2:T(2,128)(2,1)S(1)} collective-permute-done((bf16[2,2,1,768]{3,1,0,2:T(2,128)(2,1)S(1)}, bf16[2,2,1,768]{3,1,0,2:T(2,128)(2,1)S(1)}, u32[]{:S(2)}, u32[]{:S(2)}) %collective-permute-start.6) | collective-permute-done | bytes 6176 | tf_op jit(solution)/shard_map/ppermute | solution.py:26
  139.1 4.0 %collective-permute-done.7 = bf16[2,2,1,768]{3,1,0,2:T(2,128)(2,1)S(1)} collective-permute-done((bf16[2,2,1,768]{3,1,0,2:T(2,128)(2,1)S(1)}, bf16[2,2,1,768]{3,1,0,2:T(2,128)(2,1)S(1)}, u32[]{:S(2)}, u32[]{:S(2)}) %collective-permute-start.7) | collective-permute-done | bytes 6176 | tf_op jit(solution)/shard_map/ppermute | solution.py:26
  143.1 4.9 %collective-permute-done.8 = bf16[2,2,1,768]{3,1,0,2:T(2,128)(2,1)S(1)} collective-permute-done((bf16[2,2,1,768]{3,1,0,2:T(2,128)(2,1)S(1)}, bf16[2,2,1,768]{3,1,0,2:T(2,128)(2,1)S(1)}, u32[]{:S(2)}, u32[]{:S(2)}) %collective-permute-start.8) | collective-permute-done | bytes 6176 | tf_op jit(solution)/shard_map/ppermute | solution.py:26
  148.0 6.4 %collective-permute-done.9 = bf16[2,2,1,768]{3,1,0,2:T(2,128)(2,1)S(1)} collective-permute-done((bf16[2,2,1,768]{3,1,0,2:T(2,128)(2,1)S(1)}, bf16[2,2,1,768]{3,1,0,2:T(2,128)(2,1)S(1)}, u32[]{:S(2)}, u32[]{:S(2)}) %collective-permute-start.9) | collective-permute-done | bytes 6176 | tf_op jit(solution)/shard_map/ppermute | solution.py:26
  154.4 1.1 collective-permute-start.10
  155.5 5.0 %collective-permute-done.10 = bf16[2,2,1,768]{3,1,0,2:T(2,128)(2,1)S(1)} collective-permute-done((bf16[2,2,1,768]{3,1,0,2:T(2,128)(2,1)S(1)}, bf16[2,2,1,768]{3,1,0,2:T(2,128)(2,1)S(1)}, u32[]{:S(2)}, u32[]{:S(2)}) %collective-permute-start.10) | collective-permute-done | bytes 6176 | tf_op jit(solution)/shard_map/ppermute | solution.py:26
  160.6 0.8 gather_fusion
  161.4 0.7 copy.143
  162.4 0.9 copy.117
  163.4 1.5 copy.119
  164.9 1.5 copy.118
  166.5 0.7 broadcast_multiply_fusion
  167.2 57.7 %all-gather.3.cloned.1.call-done = bf16[2,2,256,1,768]{4,2,1,3,0:T(8,128)(2,1)} async-done(((bf16[2,2,16,1,768]{4,2,1,3,0:T(8,128)(2,1)}), bf16[2,2,256,1,768]{4,2,1,3,0:T(8,128)(2,1)}) %all-gather.3.cloned.1.call-update) | async-done | bytes 1572880 | tf_op jit(solution)/shard_map/all_gather | solution.py:98
  224.9 1.7 fusion.9
  226.6 1.6 fusion.1
  228.3 0.9 copy.88
  230.4 1.5 copy.87
  232.0 2.2 copy.90
  234.1 1.5 fusion.21
  237.1 0.5 subtract_convert_fusion
  238.2 2.3 fusion.10
  240.5 0.6 fusion.16
  241.2 2.3 fusion.14
  243.5 2.3 fusion.12
  245.7 3.5 %copy.102 = f32[64,2,3,16,16]{0,3,4,2,1:T(8,128)} copy(f32[64,2,3,16,16]{4,3,2,1,0:T(8,128)} %fusion.10) | data formatting | bytes 786432 | tf_op jit(solution)/shard_map/qkac,kqman->kqmcn/dot_general | solution.py:124
  249.2 2.3 copy.97
  251.5 3.7 %copy.101 = f32[64,2,3,16,16]{0,3,4,2,1:T(8,128)} copy(f32[64,2,3,16,16]{4,3,2,1,0:T(8,128)} %fusion.14) | data formatting | bytes 786432 | tf_op jit(solution)/shard_map/qkac,kqman->kqmcn/dot_general | solution.py:122
  255.2 2.3 copy.98
  257.5 2.1 fusion.7
  259.8 1.1 copy.103
  (94 shorter events, 5.7 us)
Async XLA Ops:
  6.5 218.4 %all-gather.3.cloned.1.call-start = ((), (), s32[]{:S(2)}) async-start(), calls=%async_computation | async-start | bytes 1671168 | tf_op jit(solution)/shard_map/all_gather | solution.py:98
  9.7 0.7 copy-start.10
  15.5 86.6 %copy-start.15 = (u32[256]{0:T(256)S(1)}, u32[256]{0:T(256)}, u32[]{:S(2)}) copy-start(u32[256]{0:T(256)} %constant.53) | copy-start | bytes 3076
  15.5 88.9 %copy-start.7 = (bf16[2,2,48,48]{3,2,1,0:T(8,128)(2,1)S(1)}, bf16[2,2,48,48]{3,2,1,0:T(8,128)(2,1)}, u32[]{:S(2)}) copy-start(bf16[2,2,48,48]{3,2,1,0:T(8,128)(2,1)} %param.19) | copy-start | bytes 55300
  102.1 60.0 %copy-start.12 = (s32[256,3]{0,1:T(4,128)S(1)}, s32[256,3]{0,1:T(4,128)}, u32[]{:S(2)}) copy-start(s32[256,3]{0,1:T(4,128)} %param.15) | copy-start | bytes 9220
  102.1 60.0 %copy-start.11 = (s32[64,16]{0,1:T(8,128)S(1)}, s32[64,16]{0,1:T(8,128)}, u32[]{:S(2)}) copy-start(s32[64,16]{0,1:T(8,128)} %param.22) | copy-start | bytes 12292
  102.1 60.0 %copy-start.8 = (bf16[2,64,16,16]{1,3,2,0:T(8,128)(2,1)S(1)}, bf16[2,64,16,16]{1,3,2,0:T(8,128)(2,1)}, u32[]{:S(2)}) copy-start(bf16[2,64,16,16]{1,3,2,0:T(8,128)(2,1)} %param.20) | copy-start | bytes 196612
  104.4 59.0 %copy-start.6 = (bf16[2,2,64,16,16]{2,4,3,1,0:T(8,128)(2,1)S(1)}, bf16[2,2,64,16,16]{2,4,3,1,0:T(8,128)(2,1)}, u32[]{:S(2)}) copy-start(bf16[2,2,64,16,16]{2,4,3,1,0:T(8,128)(2,1)} %param.21) | copy-start | bytes 393220
  105.5 55.1 %collective-permute-start.14 = (bf16[2,2,1,768]{3,1,0,2:T(2,128)(2,1)S(1)}, bf16[2,2,1,768]{3,1,0,2:T(2,128)(2,1)S(1)}, u32[]{:S(2)}, u32[]{:S(2)}) collective-permute-start(bf16[2,2,1,768]{3,1,0,2:T(2,128)(2,1)S(1)} %get-tuple-element.17), channel_id=1, source_target_pairs={{0,240},{16,224},{32,208},{48,192},{64,176},{80,160},{96,144},{112... | collective-permute-start | bytes 18440 | tf_op jit(solution)/shard_map/ppermute | solution.py:26
  106.7 53.9 %collective-permute-start.13 = (bf16[2,2,1,768]{3,1,0,2:T(2,128)(2,1)S(1)}, bf16[2,2,1,768]{3,1,0,2:T(2,128)(2,1)S(1)}, u32[]{:S(2)}, u32[]{:S(2)}) collective-permute-start(bf16[2,2,1,768]{3,1,0,2:T(2,128)(2,1)S(1)} %get-tuple-element.18), channel_id=1, source_target_pairs={{0,224},{16,240},{32,192},{48,208},{64,160},{80,176},{96,128},{112... | collective-permute-start | bytes 18440 | tf_op jit(solution)/shard_map/ppermute | solution.py:26
  107.4 53.1 %collective-permute-start.12 = (bf16[2,2,1,768]{3,1,0,2:T(2,128)(2,1)S(1)}, bf16[2,2,1,768]{3,1,0,2:T(2,128)(2,1)S(1)}, u32[]{:S(2)}, u32[]{:S(2)}) collective-permute-start(bf16[2,2,1,768]{3,1,0,2:T(2,128)(2,1)S(1)} %get-tuple-element.19), channel_id=1, source_target_pairs={{0,208},{16,192},{32,240},{48,224},{64,144},{80,128},{96,176},{112... | collective-permute-start | bytes 18440 | tf_op jit(solution)/shard_map/ppermute | solution.py:26
  107.4 53.1 %collective-permute-start.11 = (bf16[2,2,1,768]{3,1,0,2:T(2,128)(2,1)S(1)}, bf16[2,2,1,768]{3,1,0,2:T(2,128)(2,1)S(1)}, u32[]{:S(2)}, u32[]{:S(2)}) collective-permute-start(bf16[2,2,1,768]{3,1,0,2:T(2,128)(2,1)S(1)} %get-tuple-element.20), channel_id=1, source_target_pairs={{0,192},{16,208},{32,224},{48,240},{64,128},{80,144},{96,160},{112... | collective-permute-start | bytes 18440 | tf_op jit(solution)/shard_map/ppermute | solution.py:26
  113.3 2.5 collective-permute-start
  115.8 4.0 %collective-permute-start.1 = (bf16[2,2,1,768]{3,1,0,2:T(2,128)(2,1)S(1)}, bf16[2,2,1,768]{3,1,0,2:T(2,128)(2,1)S(1)}, u32[]{:S(2)}, u32[]{:S(2)}) collective-permute-start(bf16[2,2,1,768]{3,1,0,2:T(2,128)(2,1)S(1)} %get-tuple-element.30), channel_id=1, source_target_pairs={{0,32},{16,48},{32,0},{48,16},{64,96},{80,112},{96,64},{112,80},{1... | collective-permute-start | bytes 18440 | tf_op jit(solution)/shard_map/ppermute | solution.py:26
  119.8 3.7 %collective-permute-start.2 = (bf16[2,2,1,768]{3,1,0,2:T(2,128)(2,1)S(1)}, bf16[2,2,1,768]{3,1,0,2:T(2,128)(2,1)S(1)}, u32[]{:S(2)}, u32[]{:S(2)}) collective-permute-start(bf16[2,2,1,768]{3,1,0,2:T(2,128)(2,1)S(1)} %get-tuple-element.29), channel_id=1, source_target_pairs={{0,48},{16,32},{32,16},{48,0},{64,112},{80,96},{96,80},{112,64},{1... | collective-permute-start | bytes 18440 | tf_op jit(solution)/shard_map/ppermute | solution.py:26
  123.5 2.8 %collective-permute-start.3 = (bf16[2,2,1,768]{3,1,0,2:T(2,128)(2,1)S(1)}, bf16[2,2,1,768]{3,1,0,2:T(2,128)(2,1)S(1)}, u32[]{:S(2)}, u32[]{:S(2)}) collective-permute-start(bf16[2,2,1,768]{3,1,0,2:T(2,128)(2,1)S(1)} %get-tuple-element.28), channel_id=1, source_target_pairs={{0,64},{16,80},{32,96},{48,112},{64,0},{80,16},{96,32},{112,48},{1... | collective-permute-start | bytes 18440 | tf_op jit(solution)/shard_map/ppermute | solution.py:26
  126.3 3.4 %collective-permute-start.4 = (bf16[2,2,1,768]{3,1,0,2:T(2,128)(2,1)S(1)}, bf16[2,2,1,768]{3,1,0,2:T(2,128)(2,1)S(1)}, u32[]{:S(2)}, u32[]{:S(2)}) collective-permute-start(bf16[2,2,1,768]{3,1,0,2:T(2,128)(2,1)S(1)} %get-tuple-element.27), channel_id=1, source_target_pairs={{0,80},{16,64},{32,112},{48,96},{64,16},{80,0},{96,48},{112,32},{1... | collective-permute-start | bytes 18440 | tf_op jit(solution)/shard_map/ppermute | solution.py:26
  129.6 4.9 %collective-permute-start.5 = (bf16[2,2,1,768]{3,1,0,2:T(2,128)(2,1)S(1)}, bf16[2,2,1,768]{3,1,0,2:T(2,128)(2,1)S(1)}, u32[]{:S(2)}, u32[]{:S(2)}) collective-permute-start(bf16[2,2,1,768]{3,1,0,2:T(2,128)(2,1)S(1)} %get-tuple-element.26), channel_id=1, source_target_pairs={{0,96},{16,112},{32,64},{48,80},{64,32},{80,48},{96,0},{112,16},{1... | collective-permute-start | bytes 18440 | tf_op jit(solution)/shard_map/ppermute | solution.py:26
  134.5 4.6 %collective-permute-start.6 = (bf16[2,2,1,768]{3,1,0,2:T(2,128)(2,1)S(1)}, bf16[2,2,1,768]{3,1,0,2:T(2,128)(2,1)S(1)}, u32[]{:S(2)}, u32[]{:S(2)}) collective-permute-start(bf16[2,2,1,768]{3,1,0,2:T(2,128)(2,1)S(1)} %get-tuple-element.25), channel_id=1, source_target_pairs={{0,112},{16,96},{32,80},{48,64},{64,48},{80,32},{96,16},{112,0},{1... | collective-permute-start | bytes 18440 | tf_op jit(solution)/shard_map/ppermute | solution.py:26
  139.1 4.0 %collective-permute-start.7 = (bf16[2,2,1,768]{3,1,0,2:T(2,128)(2,1)S(1)}, bf16[2,2,1,768]{3,1,0,2:T(2,128)(2,1)S(1)}, u32[]{:S(2)}, u32[]{:S(2)}) collective-permute-start(bf16[2,2,1,768]{3,1,0,2:T(2,128)(2,1)S(1)} %get-tuple-element.24), channel_id=1, source_target_pairs={{0,128},{16,144},{32,160},{48,176},{64,192},{80,208},{96,224},{112... | collective-permute-start | bytes 18440 | tf_op jit(solution)/shard_map/ppermute | solution.py:26
  143.1 4.9 %collective-permute-start.8 = (bf16[2,2,1,768]{3,1,0,2:T(2,128)(2,1)S(1)}, bf16[2,2,1,768]{3,1,0,2:T(2,128)(2,1)S(1)}, u32[]{:S(2)}, u32[]{:S(2)}) collective-permute-start(bf16[2,2,1,768]{3,1,0,2:T(2,128)(2,1)S(1)} %get-tuple-element.23), channel_id=1, source_target_pairs={{0,144},{16,128},{32,176},{48,160},{64,208},{80,192},{96,240},{112... | collective-permute-start | bytes 18440 | tf_op jit(solution)/shard_map/ppermute | solution.py:26
  148.0 6.4 %collective-permute-start.9 = (bf16[2,2,1,768]{3,1,0,2:T(2,128)(2,1)S(1)}, bf16[2,2,1,768]{3,1,0,2:T(2,128)(2,1)S(1)}, u32[]{:S(2)}, u32[]{:S(2)}) collective-permute-start(bf16[2,2,1,768]{3,1,0,2:T(2,128)(2,1)S(1)} %get-tuple-element.22), channel_id=1, source_target_pairs={{0,160},{16,176},{32,128},{48,144},{64,224},{80,240},{96,192},{112... | collective-permute-start | bytes 18440 | tf_op jit(solution)/shard_map/ppermute | solution.py:26
  154.4 6.1 %collective-permute-start.10 = (bf16[2,2,1,768]{3,1,0,2:T(2,128)(2,1)S(1)}, bf16[2,2,1,768]{3,1,0,2:T(2,128)(2,1)S(1)}, u32[]{:S(2)}, u32[]{:S(2)}) collective-permute-start(bf16[2,2,1,768]{3,1,0,2:T(2,128)(2,1)S(1)} %get-tuple-element.21), channel_id=1, source_target_pairs={{0,176},{16,160},{32,144},{48,128},{64,240},{80,224},{96,208},{112... | collective-permute-start | bytes 18440 | tf_op jit(solution)/shard_map/ppermute | solution.py:26
  161.4 5.1 %copy-start.14 = (s32[256]{0:T(256)S(1)}, s32[256]{0:T(256)}, u32[]{:S(2)}) copy-start(s32[256]{0:T(256)} %param.16) | copy-start | bytes 3076
  161.4 5.1 %copy-start.13 = (f32[64,3]{0,1:T(4,128)S(1)}, f32[64,3]{0,1:T(4,128)}, u32[]{:S(2)}) copy-start(f32[64,3]{0,1:T(4,128)} %param.18) | copy-start | bytes 2308
  161.4 5.1 %copy-start.9 = (s32[2,64,16]{1,2,0:T(8,128)S(1)}, s32[2,64,16]{1,2,0:T(8,128)}, u32[]{:S(2)}) copy-start(s32[2,64,16]{1,2,0:T(8,128)} %param.23) | copy-start | bytes 24580
  224.9 4.3 %copy-start.1 = (bf16[2,2,256,1,768]{4,2,1,3,0:T(8,128)(2,1)S(1)}, bf16[2,2,256,1,768]{4,2,1,3,0:T(8,128)(2,1)}, u32[]{:S(2)}) copy-start(bf16[2,2,256,1,768]{4,2,1,3,0:T(8,128)(2,1)} %all-gather.3.cloned.1.call-done) | copy-start | bytes 4718596
  236.2 1.0 copy-start.4
  237.1 1.0 copy-start.2
  238.2 2.3 copy-start.3
  251.5 3.7 %copy-start = (f32[64,2,3,16,16]{4,3,2,1,0:T(8,128)S(1)}, f32[64,2,3,16,16]{4,3,2,1,0:T(8,128)}, u32[]{:S(2)}) copy-start(f32[64,2,3,16,16]{4,3,2,1,0:T(8,128)} %fusion.12) | copy-start | bytes 1179652
  255.2 2.3 copy-start.5
Sparse Core Ops, SparseCore 0:
  162.2 62.6 all-gather.2
